TPU v7x, 256 devices: a whole 4x4x8 slice. The times are simulated.
256 devices in a mesh: sec: 64 (over y, z, core), op: 4 (over x).
Axes of the slice: x: 4, y: 4, z: 8, core: 2. Of those that a mesh axis runs over, the one named last changes fastest.
Arguments:
- wave: bfloat16 [384, 256, 256], P('sec', 'op'), may hold values from -6 to 6
- left_ops: bfloat16 [384, 32, 256, 256], P('sec', 'op'), may hold values from -0.09375 to 0.09375
- right_ops: bfloat16 [384, 32, 256, 256], P('sec', 'op'), may hold values from -0.375 to 0.375
- owner_map: int32 [384, 5], P('sec'), may hold values from 0 to 63, all different within a row; in each aligned block of 6 rows (0 to 5, 6 to 11, ...) at most 2 rows name the same one
- local_map: int32 [384, 5], P('sec'), may hold values from 0 to 5
- op_class: int32 [32], P('op'), may hold values from 0 to 4
Outputs:
- applied: bfloat16 [384, 256, 256], P('sec', 'op')
Inputs may be any that keep to these rules, and one draw needn't show every extreme that they name: `owner_map`: each row names 5 different owners; among the rows of one sec index no owner is named more than 2 times, and that count is reached.
All inputs are finite; a program needn't handle non-finite values.
Results may differ from a plain program's by a relative error of at most 0.0049.
Values may be sent and summed in bfloat16 or wider, within the bound.
A program may use at most 128 MiB of HBM per device.

v0:
```python
import jax
import jax.numpy as jnp
from jax import lax
from jax.sharding import PartitionSpec as P


def shards(wave, left_ops, right_ops, owner_map, local_map, op_class):
    sec_dev, classes = owner_map.shape
    block_size = left_ops.shape[2]
    source = owner_map * sec_dev + local_map
    every_wave = lax.all_gather(wave, "sec", axis=0, tiled=True)
    compact = every_wave[source.reshape(sec_dev * classes)]
    sources = lax.all_gather(compact, "op", axis=1, tiled=True)
    sources = sources.reshape(sec_dev, classes, block_size, block_size)
    chosen = sources[:, op_class]
    lifted = jnp.einsum(
        "tonk,tokm->tonm", left_ops, chosen, preferred_element_type=jnp.float32
    ).astype(jnp.bfloat16)
    partial_value = jnp.einsum(
        "tonm,tokm->tnk", lifted, right_ops, preferred_element_type=jnp.float32
    ).astype(jnp.bfloat16)
    return lax.psum_scatter(partial_value, "op", scatter_dimension=1, tiled=True)


def solution(mesh):
    in_specs = (
        P("sec", "op", None),
        P("sec", "op", None, None),
        P("sec", "op", None, None),
        P("sec", None),
        P("sec", None),
        P("op"),
    )
    out_specs = P("sec", "op", None)
    return jax.shard_map(shards, mesh=mesh, in_specs=in_specs, out_specs=out_specs, check_vma=False)
```

profile of v0, /device:TPU:8, one launch (start us, length us, event | category | flops | bytes accessed | tf_op | source)
XLA Modules:
  0.0 203.4 jit_solution(12440562342349995092)
XLA Ops:
  6.5 0.0 all-gather.4.cloned.1.call-start
  6.5 0.7 all-gather.4.cloned.1.call-update
  7.3 0.0 all-gather.6.cloned.1.call-start
  7.3 0.7 multiply_add_fusion
  8.0 0.1 reshape.34
  8.1 93.7 %all-gather.4.cloned.1.call-done = bf16[384,64,256]{2,1,0:T(8,128)(2,1)} async-done(((bf16[6,64,256]{2,1,0:T(8,128)(2,1)}), bf16[384,64,256]{2,1,0:T(8,128)(2,1)}) %all-gather.4.cloned.1.call-update) | async-done | bytes 12582928 | tf_op jit(solution)/shard_map/all_gather | solution.py:11
  101.8 6.2 %gather_fusion = bf16[30,64,256]{2,1,0:T(8,128)(2,1)} fusion(bf16[384,64,256]{2,1,0:T(8,128)(2,1)} %all-gather.4.cloned.1.call-done, s32[1024]{0:T(1024)S(1)} %pad_clamp_fusion.1), kind=kCustom, calls=%fused_computation | custom fusion | bytes 1966200 | tf_op jit(solution)/shard_map/gather | solution.py:12
  108.0 0.0 all-gather.6.cloned.1.call-update
  108.0 0.0 reduce-scatter.2.cloned.1.call-start
  108.1 0.7 compare_select_fusion
  108.7 46.2 %all-gather.6.cloned.1.call-done = bf16[30,256,256]{2,1,0:T(8,128)(2,1)} async-done(((bf16[30,64,256]{2,1,0:T(8,128)(2,1)}), bf16[30,256,256]{2,1,0:T(8,128)(2,1)}) %all-gather.6.cloned.1.call-update) | async-done | bytes 3932176 | tf_op jit(solution)/shard_map/all_gather | solution.py:13
  154.9 5.7 %gather_fusion.1 = bf16[8,6,256,256]{3,2,1,0:T(8,128)(2,1)} fusion(bf16[6,5,256,256]{3,2,1,0:T(8,128)(2,1)} %bitcast.18, s32[1024]{0:T(1024)S(1)} %pad_clamp_fusion), kind=kCustom, calls=%fused_computation.1 | custom fusion | bytes 12582944 | tf_op jit(solution)/shard_map/gather | solution.py:15
  160.7 10.7 %bitcast_convert_fusion = bf16[6,256,256]{2,1,0:T(8,128)(2,1)} fusion(bf16[6,8,256,256]{3,2,1,0:T(8,128)(2,1)} %param.8, bf16[6,8,256,256]{3,2,1,0:T(8,128)(2,1)} %param.7, bf16[8,6,256,256]{3,2,1,0:T(8,128)(2,1)} %gather_fusion.1), kind=kOutput, calls=%fused_computation.7 | convolution fusion | flops 3224764416 | bytes 19660800 | tf_op jit(solution)/shard_map/tonm,tokm->tnk/dot_general | solution.py:19
  171.4 0.0 reduce-scatter.2.cloned.1.call-update
  171.4 25.4 %reduce-scatter.2.cloned.1.call-done = bf16[6,64,256]{2,1,0:T(8,128)(2,1)} async-done(((bf16[6,256,256]{2,1,0:T(8,128)(2,1)}), bf16[6,64,256]{2,1,0:T(8,128)(2,1)}) %reduce-scatter.2.cloned.1.call-update) | async-done | bytes 196624 | tf_op jit(solution)/shard_map/reduce_scatter | solution.py:22
  (3 shorter events, 0.0 us)
Async XLA Ops:
  6.5 95.2 %all-gather.4.cloned.1.call-start = ((), (), s32[]{:S(2)}) async-start(), calls=%async_computation.1 | async-start | bytes 12779520 | tf_op jit(solution)/shard_map/all_gather | solution.py:11
  7.3 147.7 %all-gather.6.cloned.1.call-start = ((), (), s32[]{:S(2)}) async-start(), calls=%async_computation.3 | async-start | bytes 4915200 | tf_op jit(solution)/shard_map/all_gather | solution.py:13
  108.0 88.8 %reduce-scatter.2.cloned.1.call-start = ((), (), s32[]{:S(2)}) async-start(), calls=%async_computation.2 | async-start | bytes 983040 | tf_op jit(solution)/shard_map/reduce_scatter | solution.py:22
Sparse Core Ops, SparseCore 0:
  10.1 91.6 all-gather.3
  108.1 46.7 all-gather.5
  171.5 25.2 reduce-scatter.1
where the time goes:
time: 204 us; the launch traced here: 203 us
  waiting for transfers between devices  166 us (81%)
  between operations  13.1 us (6%)
  local copies, waits for them, and re-layouts  12 us (6%)
  matrix products  10.7 us (5%)
    all_gather x1, waiting for transfers between devices, shards(): every_wave = lax.all_gather(wave, 'sec', axis=0, tiled=True)  93.7 us
    all_gather x1, waiting for transfers between devices, shards(): sources = lax.all_gather(compact, 'op', axis=1, tiled=True)  46.2 us
    reduce_scatter x1, waiting for transfers between devices, shards(): lax.psum_scatter(partial_value, 'op', scatter_dimension=1, tiled=True)  25.4 us
    dot_general x1, matrix products, shards(): jnp.einsum('tonm,tokm->tnk', lifted, right_ops, preferred_element_type=jn...  10.7 us
    gather x1, local copies, waits for them, and re-layouts, shards(): compact = every_wave[source.reshape(sec_dev * classes)]  6.22 us
    gather x1, local copies, waits for them, and re-layouts, shards(): chosen = sources[:, op_class]  5.72 us
  transfers between devices with their start and end apart: 3, of which 3 were waited for; matrix products, arithmetic and copies ran while one was open for 1% of the time, Pallas kernels for 0%

commit v1 on v0

--- a/solution.py
+++ b/solution.py
@@ -8,7 +8,11 @@
     sec_dev, classes = owner_map.shape
     block_size = left_ops.shape[2]
     source = owner_map * sec_dev + local_map
-    every_wave = lax.all_gather(wave, "sec", axis=0, tiled=True)
+    peers = lax.axis_size("sec")
+    repeats = [peers if d == 0 else 1 for d in range(wave.ndim)]
+    every_wave = lax.all_to_all(
+        jnp.tile(wave, repeats), "sec", split_axis=0, concat_axis=0, tiled=True
+    )
     compact = every_wave[source.reshape(sec_dev * classes)]
     sources = lax.all_gather(compact, "op", axis=1, tiled=True)
     sources = sources.reshape(sec_dev, classes, block_size, block_size)

time: 204 us -> 402 us (1.97)
  waiting for transfers between devices: 166 us -> 346 us
  starting transfers between devices: 0.08 us -> 12.5 us
  local copies, waits for them, and re-layouts: 12 us -> 19 us
    all_to_all x0 -> x1, waiting for transfers between devices: none -> 274 us  [shards(): lax.all_to_all(jnp.tile(wave, repeats), 'sec', split_axis=0, concat_axis=...]
    all_gather x1 -> x0, waiting for transfers between devices: 93.7 us -> none  [shards(): every_wave = lax.all_gather(wave, 'sec', axis=0, tiled=True)]
    all_to_all x0 -> x1, starting transfers between devices: none -> 12.4 us  [shards(): lax.all_to_all(jnp.tile(wave, repeats), 'sec', split_axis=0, concat_axis=...]
    another operation x0 -> x1, local copies, waits for them, and re-layouts: none -> 7.01 us  [shards(): jnp.tile(wave, repeats)]
  transfers between devices with their start and end apart: 3 -> 3, of which waited for: 3 -> 3; matrix products, arithmetic and copies ran while one was open for 1% -> 0% of each run, Pallas kernels for 0% -> 0%
where the time goes in v1:
time: 402 us
  waiting for transfers between devices  346 us (86%)
  local copies, waits for them, and re-layouts  19 us (5%)
  between operations  13.5 us (3%)
  starting transfers between devices  12.5 us (3%)
  matrix products  10.7 us (3%)
    all_to_all x1, waiting for transfers between devices, shards(): lax.all_to_all(jnp.tile(wave, repeats), 'sec', split_axis=0, concat_axis=...  274 us
    all_gather x1, waiting for transfers between devices, shards(): sources = lax.all_gather(compact, 'op', axis=1, tiled=True)  46.5 us
    reduce_scatter x1, waiting for transfers between devices, shards(): lax.psum_scatter(partial_value, 'op', scatter_dimension=1, tiled=True)  25.4 us
    all_to_all x1, starting transfers between devices, shards(): lax.all_to_all(jnp.tile(wave, repeats), 'sec', split_axis=0, concat_axis=...  12.4 us
    dot_general x1, matrix products, shards(): jnp.einsum('tonm,tokm->tnk', lifted, right_ops, preferred_element_type=jn...  10.7 us
  transfers between devices with their start and end apart: 3, of which 3 were waited for; matrix products, arithmetic and copies ran while one was open for 0% of the time, Pallas kernels for 0%

profile of v1, /device:TPU:8, one launch (start us, length us, event | category | flops | bytes accessed | tf_op | source)
XLA Modules:
  0.0 402.1 jit_solution(13526671281004678154)
XLA Ops:
  6.5 7.0 %tile.4 = bf16[64,6,64,256]{3,2,1,0:T(8,128)(2,1)} broadcast(bf16[6,64,256]{2,1,0:T(8,128)(2,1)} %param.6), dimensions={1,2,3} | broadcast | bytes 12779520 | tf_op jit(solution)/shard_map/tile | solution.py:14
  13.5 0.0 copy-start
  13.5 0.0 copy-start.1
  13.5 0.0 copy-start.2
  13.6 12.4 %all-to-all-start = ((bf16[384,64,256]{2,1,0:T(8,128)(2,1)}), bf16[384,64,256]{2,1,0:T(8,128)(2,1)}, u32[]{:S(2)}, u32[]{:S(2)}) async-start(bf16[384,64,256]{2,1,0:T(8,128)(2,1)} %bitcast.19), calls=%async_computation | async-start | bytes 25165824 | tf_op jit(solution)/shard_map/all_to_all | solution.py:13
  26.0 0.0 all-gather.3.cloned.1.call-start
  26.0 0.0 copy-done
  26.0 0.0 copy-done.1
  26.0 0.1 reshape.38
  26.1 274.4 %all-to-all-done = bf16[384,64,256]{2,1,0:T(8,128)(2,1)} async-done(((bf16[384,64,256]{2,1,0:T(8,128)(2,1)}), bf16[384,64,256]{2,1,0:T(8,128)(2,1)}, u32[]{:S(2)}, u32[]{:S(2)}) %all-to-all-start) | async-done | bytes 12582944 | tf_op jit(solution)/shard_map/all_to_all | solution.py:13
  300.5 6.2 %gather_fusion = bf16[30,64,256]{2,1,0:T(8,128)(2,1)} fusion(bf16[384,64,256]{2,1,0:T(8,128)(2,1)} %all-to-all-done, s32[1024]{0:T(1024)S(1)} %pad_clamp_fusion.1), kind=kCustom, calls=%fused_computation | custom fusion | bytes 1966200 | tf_op jit(solution)/shard_map/gather | solution.py:16
  306.7 0.0 all-gather.3.cloned.1.call-update
  306.8 0.0 reduce-scatter.2.cloned.1.call-start
  306.8 0.0 copy-done.2
  306.8 46.5 %all-gather.3.cloned.1.call-done = bf16[30,256,256]{2,1,0:T(8,128)(2,1)} async-done(((bf16[30,64,256]{2,1,0:T(8,128)(2,1)}), bf16[30,256,256]{2,1,0:T(8,128)(2,1)}) %all-gather.3.cloned.1.call-update) | async-done | bytes 3932176 | tf_op jit(solution)/shard_map/all_gather | solution.py:17
  353.4 5.7 %gather_fusion.1 = bf16[8,6,256,256]{3,2,1,0:T(8,128)(2,1)} fusion(bf16[6,5,256,256]{3,2,1,0:T(8,128)(2,1)} %bitcast.20, s32[1024]{0:T(1024)S(1)} %pad_clamp_fusion), kind=kCustom, calls=%fused_computation.1 | custom fusion | bytes 12582944 | tf_op jit(solution)/shard_map/gather | solution.py:19
  359.1 10.7 %bitcast_convert_fusion = bf16[6,256,256]{2,1,0:T(8,128)(2,1)} fusion(bf16[6,8,256,256]{3,2,1,0:T(8,128)(2,1)} %param.8, bf16[6,8,256,256]{3,2,1,0:T(8,128)(2,1)} %param.7, bf16[8,6,256,256]{3,2,1,0:T(8,128)(2,1)} %gather_fusion.1), kind=kOutput, calls=%fused_computation.7 | convolution fusion | flops 3224764416 | bytes 19660800 | tf_op jit(solution)/shard_map/tonm,tokm->tnk/dot_general | solution.py:23
  369.8 0.0 reduce-scatter.2.cloned.1.call-update
  369.9 25.4 %reduce-scatter.2.cloned.1.call-done = bf16[6,64,256]{2,1,0:T(8,128)(2,1)} async-done(((bf16[6,256,256]{2,1,0:T(8,128)(2,1)}), bf16[6,64,256]{2,1,0:T(8,128)(2,1)}) %reduce-scatter.2.cloned.1.call-update) | async-done | bytes 196624 | tf_op jit(solution)/shard_map/reduce_scatter | solution.py:26
  (5 shorter events, 0.0 us)
Async XLA Ops:
  13.5 12.5 %copy-start = (s32[6,5]{1,0:T(8,128)S(1)}, s32[6,5]{1,0:T(8,128)}, u32[]{:S(2)}) copy-start(s32[6,5]{1,0:T(8,128)} %param.10) | copy-start | bytes 364
  13.5 12.5 %copy-start.1 = (s32[6,5]{1,0:T(8,128)S(1)}, s32[6,5]{1,0:T(8,128)}, u32[]{:S(2)}) copy-start(s32[6,5]{1,0:T(8,128)} %param.9) | copy-start | bytes 364
  13.5 293.3 %copy-start.2 = (s32[8]{0:T(128)S(1)}, s32[8]{0:T(128)}, u32[]{:S(2)}) copy-start(s32[8]{0:T(128)} %param.11) | copy-start | bytes 100
  13.6 287.0 %all-to-all-start = ((bf16[384,64,256]{2,1,0:T(8,128)(2,1)}), bf16[384,64,256]{2,1,0:T(8,128)(2,1)}, u32[]{:S(2)}, u32[]{:S(2)}) async-start(bf16[384,64,256]{2,1,0:T(8,128)(2,1)} %bitcast.19), calls=%async_computation | async-start | bytes 25165824 | tf_op jit(solution)/shard_map/all_to_all | solution.py:13
  26.0 327.4 %all-gather.3.cloned.1.call-start = ((), (), s32[]{:S(2)}) async-start(), calls=%async_computation.3 | async-start | bytes 4915200 | tf_op jit(solution)/shard_map/all_gather | solution.py:17
  306.8 88.5 %reduce-scatter.2.cloned.1.call-start = ((), (), s32[]{:S(2)}) async-start(), calls=%async_computation.2 | async-start | bytes 983040 | tf_op jit(solution)/shard_map/reduce_scatter | solution.py:26
Sparse Core Ops, SparseCore 0:
  306.9 46.4 all-gather.2
  370.0 25.2 reduce-scatter.1
